TPU v7x, 256 devices: a whole 4x4x8 slice. The times are simulated.
256 devices in a mesh: ctx: 32 (over z, x), head: 8 (over y, core).
Axes of the slice: x: 4, y: 4, z: 8, core: 2. Of those that a mesh axis runs over, the one named last changes fastest.
Arguments:
- layer_input: bfloat16 [65536, 3072], P(('ctx', 'head')), may hold values from -1.1953125 to 1.1953125
- cotangent: bfloat16 [65536, 3072], P(('ctx', 'head')), may hold values from -1.1953125 to 1.1953125
- b_proj: bfloat16 [65536, 128], P('ctx'), may hold values from -0.1796875 to 0.1796875
- c_proj: bfloat16 [65536, 128], P('ctx'), may hold values from -0.1796875 to 0.1796875
- log_decay: float32 [65536, 48], P('ctx', 'head'), may hold values from -1 to 0
- resets: int32 [65536], P('ctx'), may hold values from 0 to 1, as said below
- agent_ids: int32 [65536], P('ctx'), may hold values from 0 to 63
- skip_gain: float32 [48], replicated, may hold values from 0.25 to 2.5
- agent_table: bfloat16 [64, 3072], P(None, 'head'), may hold values from -0.59765625 to 0.59765625
Outputs:
- layer_output: bfloat16 [65536, 3072], P(('ctx', 'head'))
- input_grad: bfloat16 [65536, 3072], P(('ctx', 'head'))
- b_grad: bfloat16 [65536, 128], P(('ctx', 'head'))
- c_grad: bfloat16 [65536, 128], P(('ctx', 'head'))
Inputs may be any that keep to these rules, and one draw needn't show every extreme that they name: `resets`: exactly 4 ones, one in each of 4 equal stretches of the sequence and never at a stretch's first token.
All inputs are finite; a program needn't handle non-finite values.
Results may differ from a plain program's by a relative error of at most 0.0085.
Values may be sent and summed in bfloat16 or wider, within the bound.
A program may use at most 256 MiB of HBM per device.

v0:
```python
import jax
import jax.numpy as jnp
from jax import lax
from jax.sharding import PartitionSpec as P

TRACT = 256


def prefix(part, axis, combine, identity, reverse):
    count = lax.axis_size(axis)
    place = lax.axis_index(axis)
    ahead = count - 1 - place if reverse else place
    gathered = jax.tree.map(lambda a: lax.all_gather(a, axis), part)
    state = jax.tree.map(lambda a, e: jnp.zeros_like(a) + jnp.asarray(e, a.dtype), part, identity)

    def one(step, state):
        source = count - 1 - step if reverse else step
        return combine(
            state, jax.tree.map(lambda a: lax.dynamic_index_in_dim(a, source, 0, False), gathered)
        )

    return lax.fori_loop(0, ahead, one, state)


def link(earlier, later):
    return (earlier[0] * later[0], later[0][:, None, None] * earlier[1] + later[1])


def tract_summary(inputs, grads, b_rows, c_rows, log_decay, resets):
    log_run = jnp.cumsum(log_decay, axis=0)
    resets_seen = jnp.cumsum(resets, axis=0, dtype=jnp.int32)
    log_end = log_run[-1]
    start_weight = jnp.where((resets_seen == 0)[:, None], jnp.exp(log_run), 0.0)
    end_weight = jnp.where(
        (resets_seen == resets_seen[-1])[:, None], jnp.exp(log_end[None, :] - log_run), 0.0
    )
    tract_decay = jnp.where(resets_seen[-1] == 0, jnp.exp(log_end), 0.0)
    inputs_end = (end_weight[:, :, None] * inputs).astype(jnp.bfloat16)
    grads_start = (start_weight[:, :, None] * grads).astype(jnp.bfloat16)
    tract_state = jnp.einsum("thp,tn->hpn", inputs_end, b_rows, preferred_element_type=jnp.float32)
    tract_adjoint = jnp.einsum(
        "thp,tn->hpn", grads_start, c_rows, preferred_element_type=jnp.float32
    )
    weights = (start_weight, end_weight, inputs_end, grads_start)
    return (log_run, resets_seen, weights, (tract_decay, tract_state, tract_adjoint))


def tract_intra(inputs, grads, b_rows, c_rows, log_run, resets_seen):
    length = log_run.shape[0]
    row_index = lax.broadcasted_iota(jnp.int32, (length, length), 0)
    col_index = lax.broadcasted_iota(jnp.int32, (length, length), 1)
    visible = (col_index <= row_index) & (resets_seen[:, None] == resets_seen[None, :])
    per_head = log_run.T
    log_gap = per_head[:, :, None] - per_head[:, None, :]
    decay_mask = jnp.where(visible[None], jnp.exp(jnp.minimum(log_gap, 0.0)), 0.0)
    c_dot_b = jnp.einsum("tn,sn->ts", c_rows, b_rows, preferred_element_type=jnp.float32)
    mixing = (decay_mask * c_dot_b[None]).astype(jnp.bfloat16)
    crossed = jnp.einsum("thp,shp->hts", grads, inputs, preferred_element_type=jnp.float32)
    paired = (decay_mask * crossed).astype(jnp.bfloat16)
    y_local = jnp.einsum("hts,shp->thp", mixing, inputs, preferred_element_type=jnp.float32)
    du_local = jnp.einsum("hts,thp->shp", mixing, grads, preferred_element_type=jnp.float32)
    dc_local = jnp.einsum("hts,sn->tn", paired, b_rows, preferred_element_type=jnp.float32)
    db_local = jnp.einsum("hts,tn->sn", paired, c_rows, preferred_element_type=jnp.float32)
    return (y_local, du_local, dc_local, db_local)


def tract_carry(b_rows, c_rows, weights, state_in, adjoint_in):
    exact = lax.Precision.HIGHEST
    start_weight, end_weight, inputs_end, grads_start = weights
    y_carry = start_weight[:, :, None] * jnp.einsum(
        "tn,hpn->thp", c_rows.astype(jnp.float32), state_in, precision=exact
    )
    du_carry = end_weight[:, :, None] * jnp.einsum(
        "tn,hpn->thp", b_rows.astype(jnp.float32), adjoint_in, precision=exact
    )
    dc_carry = jnp.einsum("thp,hpn->tn", grads_start.astype(jnp.float32), state_in, precision=exact)
    db_carry = jnp.einsum(
        "thp,hpn->tn", inputs_end.astype(jnp.float32), adjoint_in, precision=exact
    )
    return (y_carry, du_carry, dc_carry, db_carry)


def finish(local, carried, inputs, grads, skip_part):
    scale = skip_part[..., None, :, None]
    y_total = (local[0] + carried[0] + scale * inputs).astype(jnp.bfloat16)
    du_total = (local[1] + carried[1] + scale * grads).astype(jnp.bfloat16)
    return (y_total, du_total, local[2] + carried[2], local[3] + carried[3])


def run_core(
    inputs_tok,
    grads_tok,
    b_tok,
    c_tok,
    decay_tok,
    resets_tok,
    skip_heads,
    tract_len,
    group_size,
    scans,
):
    tokens, feature_width = inputs_tok.shape
    head_count = decay_tok.shape[1]
    head_width = feature_width // head_count
    state_size = b_tok.shape[1]
    tract_count = tokens // tract_len
    group_count = head_count // group_size
    block_count = tract_count * group_count

    def to_blocks(values):
        values = values.reshape(
            tract_count, tract_len, group_count, group_size, head_width
        ).transpose(0, 2, 1, 3, 4)
        return values.reshape(block_count, tract_len, group_size, head_width)

    def from_blocks(values):
        values = values.reshape(
            tract_count, group_count, tract_len, group_size, head_width
        ).transpose(0, 2, 1, 3, 4)
        return values.reshape(tokens, feature_width)

    def sum_groups(values):
        return (
            values.reshape(tract_count, group_count, tract_len, state_size)
            .sum(axis=1)
            .reshape(tokens, state_size)
        )

    inputs_blk = to_blocks(inputs_tok)
    grads_blk = to_blocks(grads_tok)
    decay_blk = decay_tok.reshape(tract_count, tract_len, group_count, group_size).transpose(
        0, 2, 1, 3
    )
    decay_blk = decay_blk.reshape(block_count, tract_len, group_size)
    b_tracts = b_tok.reshape(tract_count, tract_len, state_size)
    c_tracts = c_tok.reshape(tract_count, tract_len, state_size)
    reset_tracts = resets_tok.reshape(tract_count, tract_len)
    skip_blk = jnp.broadcast_to(
        skip_heads.reshape(1, group_count, group_size), (tract_count, group_count, group_size)
    )
    skip_blk = skip_blk.reshape(block_count, group_size)
    owners = jnp.arange(block_count, dtype=jnp.int32) // group_count
    records = (inputs_blk, grads_blk, decay_blk, owners)

    def fetch(record):
        inputs, grads, decays, tract_index = record
        b_rows = lax.dynamic_index_in_dim(b_tracts, tract_index, 0, keepdims=False)
        c_rows = lax.dynamic_index_in_dim(c_tracts, tract_index, 0, keepdims=False)
        flags = lax.dynamic_index_in_dim(reset_tracts, tract_index, 0, keepdims=False)
        return (inputs, grads, b_rows, c_rows, decays, flags)

    def summary_only(record):
        inputs, grads, b_rows, c_rows, decays, flags = fetch(record)
        return tract_summary(inputs, grads, b_rows, c_rows, decays, flags)[3]

    summaries = lax.map(summary_only, records)
    decays = summaries[0]
    states = summaries[1]
    adjoints = summaries[2]
    neutral = (
        jnp.ones((head_count,), jnp.float32),
        jnp.zeros((head_count, head_width, state_size), jnp.float32),
    )

    def advance(running, record):
        return (link(running, record), running)

    forward_total, forward_prefix = lax.scan(advance, neutral, (decays, states))
    backward_total, backward_prefix = lax.scan(advance, neutral, (decays, adjoints), reverse=True)
    state_from, adjoint_from = scans(forward_total, backward_total)
    state_in = forward_prefix[1] + forward_prefix[0][:, :, None, None] * state_from[None]
    adjoint_in = backward_prefix[1] + backward_prefix[0][:, :, None, None] * adjoint_from[None]
    state_blk = state_in
    adjoint_blk = adjoint_in

    def complete(bundle):
        record, state_in, adjoint_in, skip_part = bundle
        inputs, grads, b_rows, c_rows, decays, flags = fetch(record)
        log_run, resets_seen, weights, summaries = tract_summary(
            inputs, grads, b_rows, c_rows, decays, flags
        )
        local = tract_intra(inputs, grads, b_rows, c_rows, log_run, resets_seen)
        carried = tract_carry(b_rows, c_rows, weights, state_in, adjoint_in)
        return finish(local, carried, inputs, grads, skip_part)

    y_blk, du_blk, dc_blk, db_blk = lax.map(complete, (records, state_blk, adjoint_blk, skip_blk))
    return (from_blocks(y_blk), from_blocks(du_blk), sum_groups(dc_blk), sum_groups(db_blk))


def body(
    layer_input, cotangent, b_proj, c_proj, log_decay, resets, agent_ids, skip_gain, agent_table
):
    agent_count = agent_table.shape[0]
    moved_input, moved_grads = (
        lax.all_to_all(layer_input, "head", split_axis=1, concat_axis=0, tiled=True),
        lax.all_to_all(cotangent, "head", split_axis=1, concat_axis=0, tiled=True),
    )
    head_local = log_decay.shape[1]
    skip_local = lax.dynamic_slice_in_dim(
        skip_gain, lax.axis_index("head") * head_local, head_local
    )
    picker = (agent_ids[:, None] == jnp.arange(agent_count, dtype=jnp.int32)[None, :]).astype(
        jnp.bfloat16
    )
    embedded = jnp.dot(picker, agent_table, preferred_element_type=jnp.float32)
    inputs_tok = (moved_input + embedded).astype(jnp.bfloat16)

    def scans(forward, backward):
        neutral = (jnp.ones_like(forward[0]), jnp.zeros_like(forward[1]))
        arriving = prefix((forward[0], forward[1]), "ctx", link, neutral, False)
        leaving = prefix((backward[0], backward[1]), "ctx", link, neutral, True)
        return (arriving[1], leaving[1])

    y_tok, dx_tok, dc_tok, db_tok = run_core(
        inputs_tok,
        moved_grads,
        b_proj,
        c_proj,
        log_decay,
        resets,
        skip_local,
        TRACT,
        head_local,
        scans,
    )
    layer_output, input_grad = (
        lax.all_to_all(y_tok, "head", split_axis=0, concat_axis=1, tiled=True),
        lax.all_to_all(dx_tok, "head", split_axis=0, concat_axis=1, tiled=True),
    )
    b_grad, c_grad = (
        lax.psum_scatter(db_tok, "head", scatter_dimension=0, tiled=True),
        lax.psum_scatter(dc_tok, "head", scatter_dimension=0, tiled=True),
    )
    return (layer_output, input_grad, b_grad.astype(jnp.bfloat16), c_grad.astype(jnp.bfloat16))


def solution(mesh):
    return jax.shard_map(
        body,
        mesh=mesh,
        in_specs=(
            P(("ctx", "head"), None),
            P(("ctx", "head"), None),
            P("ctx", None),
            P("ctx", None),
            P("ctx", "head"),
            P("ctx"),
            P("ctx"),
            P(),
            P(None, "head"),
        ),
        out_specs=(
            P(("ctx", "head"), None),
            P(("ctx", "head"), None),
            P(("ctx", "head"), None),
            P(("ctx", "head"), None),
        ),
        check_vma=False,
    )
```

profile of v0, /device:TPU:1, one launch (start us, length us, event | category | flops | bytes accessed | tf_op | source)
XLA Modules:
  0.0 648.2 jit_solution(14824964774728890673)
XLA Ops:
  7.2 2.7 copy.100
  9.9 6.9 %all-to-all-start = ((bf16[256,8,384]{2,0,1:T(8,128)(2,1)}), bf16[256,8,384]{2,0,1:T(8,128)(2,1)S(1)}, u32[]{:S(2)}, u32[]{:S(2)}) async-start(bf16[256,8,384]{2,0,1:T(8,128)(2,1)} %bitcast.194), calls=%async_computation | async-start | bytes 3145728 | tf_op jit(solution)/shard_map/all_to_all | solution.py:195
  18.3 19.2 %all-to-all-done = bf16[256,8,384]{2,0,1:T(8,128)(2,1)S(1)} async-done(((bf16[256,8,384]{2,0,1:T(8,128)(2,1)}), bf16[256,8,384]{2,0,1:T(8,128)(2,1)S(1)}, u32[]{:S(2)}, u32[]{:S(2)}) %all-to-all-start) | async-done | bytes 1572896 | tf_op jit(solution)/shard_map/all_to_all | solution.py:195
  37.5 4.5 all-to-all-start.1
  47.6 15.2 %all-to-all-done.1 = bf16[256,8,384]{0,2,1:T(8,128)(2,1)S(1)} async-done(((bf16[256,8,384]{0,2,1:T(8,128)(2,1)}), bf16[256,8,384]{0,2,1:T(8,128)(2,1)S(1)}, u32[]{:S(2)}, u32[]{:S(2)}) %all-to-all-start.1) | async-done | bytes 1572896 | tf_op jit(solution)/shard_map/all_to_all | solution.py:196
  65.4 95.3 %while.94 = (s32[]{:T(128)}, f32[8,6]{1,0:T(8,128)S(1)}, f32[8,6,64,128]{3,2,1,0:T(8,128)}, f32[8,6,64,128]{3,2,1,0:T(8,128)}, s32[8]{0:T(128)S(1)}, /*index=5*/...) while((s32[]{:T(128)}, f32[8,6]{1,0:T(8,128)S(1)}, ...), condition=%wide.region_5.6_spmd, body=%wide.region_0.5_spmd.sunk | while | flops 51156000 | bytes 1047529 | solution.py:156
  160.9 9.0 %while.98 = (s32[]{:T(128)}, f32[6]{0:T(128)S(1)}, f32[6,64,128]{2,1,0:T(8,128)S(1)}, f32[8,6]{1,0:T(8,128)S(1)}, f32[8,6,64,128]{3,2,1,0:T(8,128)S(1)}, /*index...) while((s32[]{:T(128)}, f32[6]{0:T(128)S(1)}, ...), condition=%wide.region_7.8_spmd.clone, body=%wide.region_6.7_spmd.clone.sunk | while | flops 196623 | bytes 983353 | solution.py:168
  172.0 14.3 %while.99 = (s32[]{:T(128)}, f32[6]{0:T(128)S(1)}, f32[6,64,128]{2,1,0:T(8,128)S(1)}, f32[8,6]{1,0:T(8,128)S(1)}, f32[8,6,64,128]{3,2,1,0:T(8,128)}, /*index=5*/...) while((s32[]{:T(128)}, f32[6]{0:T(128)S(1)}, ...), condition=%wide.region_11.12_spmd.clone, body=%wide.region_10.11_spmd.clone.sunk | while | flops 196624 | bytes 983373 | solution.py:169
  189.0 63.5 %all-reduce.2 = (f32[192]{0:T(256)S(1)}, f32[192]{0:T(256)S(1)}) all-reduce(f32[192]{0:T(256)S(1)} %dynamic-update-slice, f32[192]{0:T(256)S(1)} %dynamic-update-slice.1), channel_id=2, replica_groups=mesh['ctx'=32,'head'=8] {'ctx'}, use_global_device_ids=true, to_apply=%add | all-reduce | flops 384 | bytes 3072
  252.7 7.1 %all-gather.7.cloned.1.call-done = f32[192,64,128]{2,1,0:T(8,128)} async-done(((f32[6,64,128]{2,1,0:T(8,128)}), f32[192,64,128]{2,1,0:T(8,128)}) %all-gather.7.cloned.1.call-update) | async-done | bytes 6291472 | tf_op jit(solution)/shard_map/all_gather | solution.py:13
  259.8 88.3 %all-gather.9.cloned.1.call-done = f32[192,64,128]{2,1,0:T(8,128)} async-done(((f32[6,64,128]{2,1,0:T(8,128)}), f32[192,64,128]{2,1,0:T(8,128)}) %all-gather.9.cloned.1.call-update) | async-done | bytes 6291472 | tf_op jit(solution)/shard_map/all_gather | solution.py:13
  348.2 33.3 %while.96 = (s32[]{:T(128)}, f32[6,64,128]{2,1,0:T(8,128)S(1)}, s32[]{:T(128)}, f32[32,6]{1,0:T(8,128)S(1)}, f32[32,6,64,128]{3,2,1,0:T(8,128)}, /*index=5*/s32[]{:T(128)}, s32[]{:T(128)}, s32[]{:T(128)}, s32[]{:T(128)}) while((s32[]{:T(128)}, f32[6,64,128]{2,1,0:T(8,128)S(1)}, s32[]{:T(128)}, f32[32,6]{1,0:T(8,128)S(1)}, ...), condition=%wide.region_13.14_spmd, body=%wide.region_12.13_spmd.sunk | while | flops 98310 | bytes 590043 | solution.py:22
  381.5 3.9 multiply_add_fusion
  385.4 182.6 %while.97 = (s32[]{:T(128)}, bf16[8,256,6,64]{1,3,2,0:T(8,128)(2,1)}, bf16[8,256,6,64]{1,3,2,0:T(8,128)(2,1)}, f32[8,256,128]{2,1,0:T(8,128)}, f32[8,256,128]{2,...) while((s32[]{:T(128)}, ...), condition=%wide.region_20.21_spmd, body=%wide.region_14.20_spmd.sunk | while | flops 814191616 | bytes 7157283 | solution.py:186
  394.9 2.0 fusion.155
  398.4 2.1 fusion.154
  417.7 2.0 fusion.155
  421.3 2.1 fusion.154
  440.5 2.0 fusion.155
  444.1 2.1 fusion.154
  466.9 2.1 fusion.154
  489.7 2.1 fusion.154
  512.6 2.1 fusion.154
  535.4 2.1 fusion.154
  558.2 2.1 fusion.154
  568.0 2.6 copy.86
  570.6 5.5 all-to-all-start.2
  578.2 22.5 %all-to-all-done.2 = bf16[8,256,384]{2,1,0:T(8,128)(2,1)S(1)} async-done(((bf16[8,256,384]{2,1,0:T(8,128)(2,1)}), bf16[8,256,384]{2,1,0:T(8,128)(2,1)S(1)}, u32[]{:S(2)}, u32[]{:S(2)}) %all-to-all-start.2) | async-done | bytes 1572896 | tf_op jit(solution)/shard_map/all_to_all | solution.py:227
  600.7 4.2 all-to-all-start.3
  606.5 2.6 copy.90
  609.1 18.3 %all-to-all-done.3 = bf16[8,256,384]{2,1,0:T(8,128)(2,1)S(1)} async-done(((bf16[8,256,384]{2,1,0:T(8,128)(2,1)}), bf16[8,256,384]{2,1,0:T(8,128)(2,1)S(1)}, u32[]{:S(2)}, u32[]{:S(2)}) %all-to-all-start.3) | async-done | bytes 1572896 | tf_op jit(solution)/shard_map/all_to_all | solution.py:228
  631.5 8.6 %reduce-scatter.5.cloned.1.call-done = f32[256,128]{1,0:T(8,128)} async-done(((f32[2048,128]{1,0:T(8,128)}), f32[256,128]{1,0:T(8,128)}) %reduce-scatter.5.cloned.1.call-update) | async-done | bytes 131088 | tf_op jit(solution)/shard_map/reduce_scatter | solution.py:232
  (681 shorter events, 297.6 us)
Async XLA Ops:
  7.2 34.9 %copy-start = (bf16[64,384]{1,0:T(8,128)(2,1)S(1)}, bf16[64,384]{1,0:T(8,128)(2,1)}, u32[]{:S(2)}) copy-start(bf16[64,384]{1,0:T(8,128)(2,1)} %param.29) | copy-start | bytes 147460
  9.9 6.9 %copy-start.4 = (bf16[256,3072]{1,0:T(8,128)(2,1)S(1)}, bf16[256,3072]{1,0:T(8,128)(2,1)}, u32[]{:S(2)}) copy-start(bf16[256,3072]{1,0:T(8,128)(2,1)} %param.22) | copy-start | bytes 4718596
  9.9 27.6 %all-to-all-start = ((bf16[256,8,384]{2,0,1:T(8,128)(2,1)}), bf16[256,8,384]{2,0,1:T(8,128)(2,1)S(1)}, u32[]{:S(2)}, u32[]{:S(2)}) async-start(bf16[256,8,384]{2,0,1:T(8,128)(2,1)} %bitcast.194), calls=%async_computation | async-start | bytes 3145728 | tf_op jit(solution)/shard_map/all_to_all | solution.py:195
  37.5 4.5 copy-start.7
  37.5 4.5 copy-start.6
  37.5 25.2 %all-to-all-start.1 = ((bf16[256,8,384]{0,2,1:T(8,128)(2,1)}), bf16[256,8,384]{0,2,1:T(8,128)(2,1)S(1)}, u32[]{:S(2)}, u32[]{:S(2)}) async-start(bf16[256,8,384]{0,2,1:T(8,128)(2,1)} %bitcast.56), calls=%async_computation.1 | async-start | bytes 3145728 | tf_op jit(solution)/shard_map/all_to_all | solution.py:196
  42.0 217.8 %all-gather.7.cloned.1.call-start = ((), (), s32[]{:S(2)}) async-start(), calls=%async_computation.8 | async-start | bytes 6488064 | tf_op jit(solution)/shard_map/all_gather | solution.py:13
  169.9 0.7 copy-start.1
  169.9 2.1 copy-start.3
  170.6 177.6 %all-gather.9.cloned.1.call-start = ((), (), s32[]{:S(2)}) async-start(), calls=%async_computation.9 | async-start | bytes 6488064 | tf_op jit(solution)/shard_map/all_gather | solution.py:13
  172.0 15.2 %copy-start.9 = (u32[256]{0:T(256)S(1)}, u32[256]{0:T(256)}, u32[]{:S(2)}) copy-start(u32[256]{0:T(256)} %constant.202) | copy-start | bytes 3076
  172.0 16.5 %copy-start.8 = (f32[48]{0:T(128)S(1)}, f32[48]{0:T(128)}, u32[]{:S(2)}) copy-start(f32[48]{0:T(128)} %param.28) | copy-start | bytes 580
  186.3 0.7 copy-start.2
  187.1 442.9 %reduce-scatter.3.cloned.1.call-start = ((), (), s32[]{:S(2)}) async-start(), calls=%async_computation.6 | async-start | bytes 1179648 | tf_op jit(solution)/shard_map/reduce_scatter | solution.py:231
  570.6 6.0 copy-start.5
  570.6 30.1 %all-to-all-start.2 = ((bf16[8,256,384]{2,1,0:T(8,128)(2,1)}), bf16[8,256,384]{2,1,0:T(8,128)(2,1)S(1)}, u32[]{:S(2)}, u32[]{:S(2)}) async-start(bf16[8,256,384]{2,1,0:T(8,128)(2,1)} %copy.86), calls=%async_computation.2 | async-start | bytes 3145728 | tf_op jit(solution)/shard_map/all_to_all | solution.py:227
  576.0 64.1 %reduce-scatter.5.cloned.1.call-start = ((), (), s32[]{:S(2)}) async-start(), calls=%async_computation.7 | async-start | bytes 1179648 | tf_op jit(solution)/shard_map/reduce_scatter | solution.py:232
  600.7 26.8 %all-to-all-start.3 = ((bf16[8,256,384]{2,1,0:T(8,128)(2,1)}), bf16[8,256,384]{2,1,0:T(8,128)(2,1)S(1)}, u32[]{:S(2)}, u32[]{:S(2)}) async-start(bf16[8,256,384]{2,1,0:T(8,128)(2,1)} %copy.88), calls=%async_computation.3 | async-start | bytes 3145728 | tf_op jit(solution)/shard_map/all_to_all | solution.py:228
Sparse Core Ops, SparseCore 0:
  170.7 89.0 all-gather.6
  262.4 85.7 all-gather.8
  568.1 31.1 reduce-scatter.2
  601.7 38.3 reduce-scatter.4
where the time goes:
time: 654 us; the launch traced here: 648 us
  waiting for transfers between devices  180 us (28%)
  matrix products  149 us (23%)
  other arithmetic  112 us (17%)
  local copies, waits for them, and re-layouts  69.9 us (11%)
  blocking collectives  63.5 us (10%)
  loops' own time  37.8 us (6%)
  starting transfers between devices  21.1 us (3%)
  between operations  14.7 us (2%)
    all_gather x2, waiting for transfers between devices, prefix(): gathered = jax.tree.map(lambda a: lax.all_gather(a, axis), part)  95.5 us
    unnamed x1, blocking collectives  63.5 us
    add x47, other arithmetic, link(): later[0][:, None, None] * earlier[1] + later[1]  48.1 us
    another operation x76, other arithmetic  35.7 us
    all_to_all x1, waiting for transfers between devices, body(): lax.all_to_all(y_tok, 'head', split_axis=0, concat_axis=1, tiled=True)  22.5 us
    another operation x1, loops' own time, run_core(): summaries = lax.map(summary_only, records)  20 us
    all_to_all x1, waiting for transfers between devices, body(): lax.all_to_all(layer_input, 'head', split_axis=1, concat_axis=0, tiled=True)  19.2 us
    another operation x137, local copies, waits for them, and re-layouts  19.1 us
  transfers between devices with their start and end apart: 8, of which 7 were waited for; matrix products, arithmetic and copies ran while one was open for 6% of the time, Pallas kernels for 0%

commit v1 on v0

v1 whole, which is shorter than its diff:
```python
import functools

import jax
import jax.numpy as jnp
from jax import lax
from jax.experimental import pallas as pl
from jax.experimental.pallas import tpu as pltpu
from jax.sharding import PartitionSpec as P

MESH = pl.DeviceIdType.MESH
F32 = jnp.float32
BF16 = jnp.bfloat16
TOK = 256
FEAT = 3072
STATE = 128
GROUP = 384
SLICE = 768
HALF = 64
PIECE = 16
CHUNKS = 2
LOG2E = 1.4426950408889634


def dot(a, b):
    return jnp.dot(a, b, preferred_element_type=F32)


def dot_nt(a, b):
    return lax.dot_general(a, b, (((1,), (1,)), ((), ())), preferred_element_type=F32)


def dot_tn(a, b):
    return lax.dot_general(a, b, (((0,), (0,)), ((), ())), preferred_element_type=F32)


def split3(a):
    hi = a.astype(BF16)
    rest = a - hi.astype(F32)
    mid = rest.astype(BF16)
    low = (rest - mid.astype(F32)).astype(BF16)
    return hi, mid, low


def kernel(
    x_hbm, g_hbm, b_hbm, c_hbm, ld_hbm, tab_hbm, resets_ref, ids_ref, skip_ref,
    out, proj_out,
    x, g, cb, cbt, ld, tab, logs, cbm, vis, paired, onehot, wcat, spread,
    u, gi, wts, loc, acc, sa, own_d, partner_sa, partner_d,
    tot, tot_d, yin, yin_d, ypre, gt, gd, xin, xin_d, xpre, rt, rd, zin, zin_d,
    xo, gc, yo, w, full,
    lsem, hs, hr, ps, pr, pds, pdr, y1s, y1r, yds, ydr, x1s, x1r, xds, xdr, z1s, z1r, zds, zdr,
    x2s, x2r, y2s, y2r, p2s, p2r, ready, ld_own,
):
    cx = lax.axis_index("ctx")
    hd = lax.axis_index("head")
    zz, xx = cx // 4, cx % 4
    yy, core = hd // 2, hd % 2
    mydir = 1 - core
    pos_y = core * yy + (1 - core) * (3 - yy)
    pos_x = core * xx + (1 - core) * (3 - xx)
    pos_z = core * zz + (1 - core) * (7 - zz)

    def at4(q):
        return core * q + (1 - core) * (3 - q)

    def at8(q):
        return core * q + (1 - core) * (7 - q)

    def remote(src, dst, s, r, dev):
        return pltpu.make_async_remote_copy(
            src_ref=src, dst_ref=dst, send_sem=s, recv_sem=r, device_id=dev, device_id_type=MESH
        )

    def half(i):
        return pl.ds(i * HALF, HALF)

    def piece(i, place):
        return pl.ds(pl.multiple_of(i * HALF + place * PIECE, PIECE), PIECE)

    ld[:, 6:8, :] = jnp.zeros((8, 2, TOK), F32)
    zin_d[...] = jnp.zeros_like(zin_d)
    zin[...] = jnp.zeros_like(zin)

    barrier = pltpu.get_barrier_semaphore()
    for k in (2, 6, 1, 7):
        pl.semaphore_signal(barrier, inc=1, device_id=(((zz + k) % 8) * 4 + xx, hd), device_id_type=MESH)
    for k in range(1, 8):
        pl.semaphore_signal(barrier, inc=1, device_id=(cx, (hd + k) % 8), device_id_type=MESH)
    for k in range(1, 4):
        pl.semaphore_signal(barrier, inc=1, device_id=(zz * 4 + (xx + k) % 4, hd), device_id_type=MESH)

    mine = pl.ds(pl.multiple_of(hd * TOK, TOK), TOK)
    own_ld = pltpu.make_async_copy(ld_hbm, ld_own, lsem.at[5])
    loads = [
        pltpu.make_async_copy(g_hbm, g, lsem.at[0]),
        pltpu.make_async_copy(b_hbm.at[mine, :], cb.at[1], lsem.at[1]),
        pltpu.make_async_copy(c_hbm.at[mine, :], cb.at[0], lsem.at[2]),
        pltpu.make_async_copy(x_hbm, x, lsem.at[3]),
    ]
    own_tab = pltpu.make_async_copy(tab_hbm, tab.at[hd], lsem.at[4])
    own_ld.start()
    own_tab.start()
    for one in (loads[1], loads[2], loads[0], loads[3]):
        one.start()

    paired[...] = jnp.zeros_like(paired)

    def build(j, carry):
        r3 = lax.broadcasted_iota(jnp.int32, (192, GROUP), 0)
        c3 = lax.broadcasted_iota(jnp.int32, (192, GROUP), 1)
        spread[:, pl.ds(pl.multiple_of(j * GROUP, 128), GROUP)] = (
            ((r3 & 63) == 8 * j + (c3 >> 6)).astype(F32).astype(BF16)
        )
        return carry

    lax.fori_loop(0, 8, build, 0)
    own_ld.wait()
    own_tab.wait()
    pl.semaphore_wait(barrier, 14)

    def ld_copy(k):
        to = (hd + k) % 8
        theirs = pl.ds(pl.multiple_of(to * TOK, TOK), TOK)
        return remote(
            ld_own.at[:, theirs], ld.at[hd, pl.ds(0, 6), :], hs.at[0, k - 1], hr.at[0, k - 1], (cx, to)
        )

    def tab_copy(k):
        return remote(tab.at[hd], tab.at[hd], hs.at[1, k - 1], hr.at[1, k - 1], (cx, (hd + k) % 8))

    for k in (4, 3, 5, 2, 6, 1, 7):
        ld_copy(k).start()
    for k in (4, 3, 5, 2, 6, 1, 7):
        tab_copy(k).start()
    for k in (2, 6):
        pl.semaphore_signal(ready, inc=1, device_id=(((zz + k) % 8) * 4 + xx, hd), device_id_type=MESH)
    ld[hd, 0:6, :] = ld_own[:, mine]

    row = lax.broadcasted_iota(jnp.int32, (TOK, TOK), 0)
    col = lax.broadcasted_iota(jnp.int32, (TOK, TOK), 1)
    upper = (row <= col).astype(F32).astype(BF16)
    flags = resets_ref[:, mine].astype(F32)
    seen = dot(jnp.broadcast_to(flags, (8, TOK)).astype(BF16), upper)
    seen_row = seen[0:1, :]
    seen_col = jnp.transpose(seen)[:, 0:1]
    visible = ((col <= row) & (seen_row == seen_col)).astype(F32)
    vis[...] = visible
    loads[1].wait()
    loads[2].wait()
    cbm[...] = dot_nt(cb[0], cb[1]) * visible
    cbt[0] = jnp.transpose(cb[0].astype(F32)).astype(BF16)
    cbt[1] = jnp.transpose(cb[1].astype(F32)).astype(BF16)
    agent = lax.broadcasted_iota(jnp.int32, (64, TOK), 0)
    picked = (agent == ids_ref[:, mine]).astype(F32)
    onehot[...] = jnp.transpose(picked).astype(BF16)

    for k in range(1, 8):
        ld_copy(k).wait_recv()
    hi, mid, low = split3(ld[...].reshape(64, TOK))
    run = (dot(hi, upper) + dot(mid, upper) + dot(low, upper)) * LOG2E
    logs[...] = run.reshape(8, 8, TOK)
    run_end = run[:, TOK - 1 : TOK]
    seen_end = seen_row[:, TOK - 1 : TOK]
    start = jnp.where(seen_row == 0, jnp.exp2(run), 0.0)
    end = jnp.where(seen_row == seen_end, jnp.exp2(jnp.minimum(run_end - run, 0.0)), 0.0)
    for index, value in ((0, start), (1, end)):
        turned = jnp.transpose(value)
        wcat[index] = jnp.concatenate(split3(turned), axis=1)

    loads[0].wait()

    def columns(j):
        return pl.ds(pl.multiple_of(j * GROUP, 128), GROUP)

    def prepare_adjoint(j, carry):
        cols = columns(j)
        weight = dot(wcat[0], spread[:, cols])
        own_d[:, cols] = weight[TOK - 1 : TOK, :]
        starts = (weight * g[:, cols].astype(F32)).astype(BF16)
        part = pl.ds(pl.multiple_of((j % 2) * GROUP, 128), GROUP)
        sa[1, j // 2, :, part] = dot(cbt[0], starts).astype(BF16)
        return carry

    lax.fori_loop(0, 8, prepare_adjoint, 0)

    partner = (cx, yy * 2 + 1 - core)

    def p0(j):
        return remote(sa.at[core, j], partner_sa.at[j], ps.at[j], pr.at[j], partner)

    def p0_d():
        return remote(own_d, partner_d, pds.at[0], pdr.at[0], partner)

    p0_d().start()

    @pl.when(core == 1)
    def _():
        for j in range(4):
            p0(j).start()

    loads[3].wait()
    for k in range(1, 8):
        tab_copy(k).wait_recv()

    def y1(i, k):
        to = at4((pos_y + k) % 4)
        return remote(
            tot.at[to, half(i), :], yin.at[pos_y, half(i), :], y1s.at[i, k - 1], y1r.at[i, k - 1], (cx, to * 2 + core)
        )

    def y1_d(k):
        to = at4((pos_y + k) % 4)
        return remote(tot_d.at[to], yin_d.at[pos_y], yds.at[k - 1], ydr.at[k - 1], (cx, to * 2 + core))

    def x1(i, k):
        to = at4((pos_x + k) % 4)
        return remote(
            gt.at[piece(i, to), :], xin.at[i, pos_x], x1s.at[i, k - 1], x1r.at[i, k - 1], (zz * 4 + to, hd)
        )

    def x1_d(k):
        to = at4((pos_x + k) % 4)
        return remote(gd, xin_d.at[pos_x], xds.at[k - 1], xdr.at[k - 1], (zz * 4 + to, hd))

    def z1(i, k):
        to = at8((pos_z + k) % 8)
        return remote(rt.at[i], zin.at[i, k - 1], z1s.at[i, k - 1], z1r.at[i, k - 1], (to * 4 + xx, hd))

    def z1_d(k):
        to = at8((pos_z + k) % 8)
        return remote(rd, zin_d.at[k - 1], zds.at[k - 1], zdr.at[k - 1], (to * 4 + xx, hd))

    def x2(i, k):
        to = (pos_x + k) % 4
        return remote(
            xo.at[i, to], gc.at[piece(i, xx), :], x2s.at[i, k - 1], x2r.at[i, k - 1], (zz * 4 + at4(to), hd)
        )

    def y2(i, k):
        to = (pos_y + k) % 4
        return remote(
            yo.at[to, half(i), :], w.at[yy, half(i), :], y2s.at[i, k - 1], y2r.at[i, k - 1], (cx, at4(to) * 2 + core)
        )

    def came(k):
        return at4((pos_y - k + 4) % 4)

    def p2(i, k):
        j = came(k)
        return remote(w.at[j, half(i), :], full.at[mydir, j, half(i), :], p2s.at[i, k], p2r.at[i, k], partner)

    def total(i):
        if i == 0:
            p0_d().wait_recv()
        for k in (2, 1, 3, 0):
            to = at4((pos_y + k) % 4)
            at = pl.ds(pl.multiple_of(to * SLICE, 128), SLICE)
            d = own_d[:, at]
            if i == 0:
                p0(to).wait_recv()
            value = (
                d * partner_sa[to, half(i), :].astype(F32) + sa[mydir, to, half(i), :].astype(F32)
            ).astype(BF16)
            if k:
                tot[to, half(i), :] = value
                y1(i, k).start()
            else:
                yin[pos_y, half(i), :] = value
            if i == 0:
                both = d * partner_d[:, at]
                if k:
                    tot_d[to] = both
                    y1_d(k).start()
                else:
                    yin_d[pos_y] = both

    def group_y(i):
        for k in (1, 3, 2):
            y1(i, k).wait_recv()
            if i == 0:
                y1_d(k).wait_recv()

        def chunk(n, carry):
            rows = piece(i, n)
            held = yin[0, rows, :].astype(F32)
            for p in range(1, 4):
                ypre[p - 1, rows, :] = held
                held = yin_d[p] * held + yin[p, rows, :].astype(F32)
            gt[rows, :] = held.astype(BF16)
            return carry

        lax.fori_loop(0, 4, chunk, 0)
        if i == 0:
            gd[...] = yin_d[0] * yin_d[1] * yin_d[2] * yin_d[3]
        for k in (2, 1, 3):
            x1(i, k).start()
        if i == 0:
            for k in (2, 1, 3):
                x1_d(k).start()
            xin_d[pos_x] = gd[...]
        xin[i, pos_x] = gt[piece(i, xx), :]

    def group_x(i):
        for k in (1, 3, 2):
            x1(i, k).wait_recv()
            if i == 0:
                x1_d(k).wait_recv()
        held = xin[i, 0].astype(F32)
        for p in range(1, 4):
            xpre[i, p - 1] = held
            held = xin_d[p] * held + xin[i, p].astype(F32)
        rt[i] = held.astype(BF16)
        if i == 0:
            rd[...] = xin_d[0] * xin_d[1] * xin_d[2] * xin_d[3]
        if i == 0:
            pl.semaphore_wait(ready, 2)
        for k in (4, 3, 5, 2, 6, 1, 7):

            @pl.when(pos_z + k < 8)
            def _():
                z1(i, k).start()
                if i == 0:
                    z1_d(k).start()

    def back_x(i):
        for k in range(1, 8):

            @pl.when(pos_z >= k)
            def _():
                z1(i, k).wait_recv()
                if i == 0:
                    z1_d(k).wait_recv()

        held = zin[i, 0].astype(F32)
        weight = zin_d[0]
        for k in range(1, 7):
            held = held + weight * zin[i, k].astype(F32)
            weight = weight * zin_d[k]
        xo[i, 0] = held.astype(BF16)
        prod = xin_d[0]
        for p in range(1, 4):
            xo[i, p] = (prod * held + xpre[i, p - 1]).astype(BF16)
            prod = prod * xin_d[p]
        for k in (2, 1, 3):
            x2(i, k).start()
        gc[piece(i, xx), :] = xo[i, pos_x]

    def back_y(i):
        for k in (1, 3, 2):
            x2(i, k).wait_recv()

        def chunk(n, carry):
            rows = piece(i, n)
            base = gc[rows, :].astype(F32)
            yo[0, rows, :] = gc[rows, :]
            prod = yin_d[0]
            for p in range(1, 4):
                yo[p, rows, :] = (prod * base + ypre[p - 1, rows, :]).astype(BF16)
                prod = prod * yin_d[p]
            return carry

        lax.fori_loop(0, 4, chunk, 0)
        for k in (2, 1, 3):
            y2(i, k).start()
        w[yy, half(i), :] = yo[pos_y, half(i), :]

    def arrive(i, k):
        if k:
            y2(i, k).wait_recv()
        p2(i, k).start()
        j = came(k)
        at = pl.ds(pl.multiple_of(j * SLICE, 128), SLICE)
        full[mydir, j, half(i), :] = (
            partner_d[:, at] * w[j, half(i), :].astype(F32) + partner_sa[j, half(i), :].astype(F32)
        ).astype(BF16)

    def finish(way, j):
        at = pl.ds(pl.multiple_of(j * SLICE, 128), SLICE)
        carried = full[way, j]
        out[way, :, at] = (loc[way, :, at] + wts[way, :, at] * dot(cb[way], carried)).astype(BF16)
        acc[way] += dot_nt(gi[way, :, at], carried)

    @pl.when(core == 0)
    def _():
        total(0)
        total(1)

    def prepare_state(n, carry):
        turn = n // 2
        step = jnp.where(turn == 0, 2, jnp.where(turn == 1, 1, jnp.where(turn == 2, 3, 0)))
        j = (yy + step) % 4
        group = j * 2 + n % 2
        cols = columns(group)
        inputs = (x[:, cols].astype(F32) + dot(onehot[...], tab[group])).astype(BF16)
        u[:, cols] = inputs
        ends = (dot(wcat[1], spread[:, cols]) * inputs.astype(F32)).astype(BF16)
        part = pl.ds(pl.multiple_of((n % 2) * GROUP, 128), GROUP)
        sa[0, j, :, part] = dot(cbt[1], ends).astype(BF16)

        @pl.when((core == 0) & (n % 2 == 1))
        def _():
            p0(j).start()

        return carry

    lax.fori_loop(0, 8, prepare_state, 0)

    @pl.when(core == 1)
    def _():
        total(0)
        total(1)

    lane = lax.broadcasted_iota(jnp.int32, (TOK, 128), 1)
    first = lane < 64

    def intra(j, carry):
        for adjoint_at, state_at, act, part in (
            (2, 4, group_y, 0),
            (4, 6, group_y, 1),
            (4, 6, group_x, 0),
            (6, 8, group_x, 1),
        ):
            pl.when(j == core * state_at + mydir * adjoint_at)(functools.partial(act, part))
        pl.when(j < 8)(functools.partial(local, j))
        return carry

    def local(j):
        rows_l = logs[j]
        cols_l = jnp.transpose(rows_l)
        for pair in range(3):
            cols = pl.ds(pl.multiple_of(j * GROUP + pair * 128, 128), 128)
            up = u[:, cols]
            gp = g[:, cols]
            for way, values in ((0, gp), (1, up)):
                weight = dot(wcat[way], spread[:, cols])
                wts[way, :, cols] = weight
                gi[way, :, cols] = (weight * values.astype(F32)).astype(BF16)
            zero = jnp.zeros_like(gp)
            ys, dus = [], []
            for side in range(2):
                r = pair * 2 + side
                lr = rows_l[r : r + 1, :]
                lc = cols_l[:, r : r + 1]
                gm = jnp.where(first, gp, zero) if side == 0 else jnp.where(first, zero, gp)
                da = jnp.exp2(jnp.minimum(lc[:128] - lr[:, :128], 0.0))
                mix_a = (da * cbm[:128, :128]).astype(BF16)
                paired[:128, :128] += da * dot_nt(gm[:128], up[:128])
                db = jnp.exp2(jnp.minimum(lc[128:] - lr, 0.0))
                mix_b = (db * cbm[128:, :]).astype(BF16)
                paired[128:, :] += db * dot_nt(gm[128:], up)
                ys.append((dot(mix_a, up[:128]), dot(mix_b, up)))
                low = dot_tn(mix_b, gp[128:])
                dus.append((low[:128] + dot_tn(mix_a, gp[:128]), low[128:]))
            s0 = skip_ref[j * 6 + pair * 2]
            s1 = skip_ref[j * 6 + pair * 2 + 1]
            scale = jnp.where(first[:128], s0, s1)
            for part in range(2):
                at = slice(part * 128, part * 128 + 128)
                loc[0, at, cols] = jnp.where(first[at], ys[0][part], ys[1][part]) + scale * up[at].astype(F32)
                loc[1, at, cols] = jnp.where(first[at], dus[0][part], dus[1][part]) + scale * gp[at].astype(F32)

    lax.fori_loop(0, 9, intra, 0)

    pairs = (paired[...] * vis[...]).astype(BF16)
    acc[0] = dot(pairs, cb[1])
    acc[1] = dot_tn(pairs, cb[0])

    back_x(0)
    back_x(1)
    back_y(0)
    back_y(1)

    def carried_here(way):
        for k in range(4):
            arrive(0, k)
        for k in range(4):
            arrive(1, k)
            finish(way, came(k))

    def carried_there(way):
        for k in range(4):
            p2(0, k).wait_recv()
            p2(1, k).wait_recv()
            finish(way, at4((pos_y + k) % 4))

    @pl.when(core == 0)
    def _():
        carried_here(1)
        carried_there(0)

    @pl.when(core == 1)
    def _():
        carried_there(1)
        carried_here(0)

    proj_out[...] = acc[...].astype(BF16)

    for k in range(1, 8):
        ld_copy(k).wait_send()
        tab_copy(k).wait_send()

        @pl.when(pos_z + k < 8)
        def _():
            z1_d(k).wait_send()
            for i in range(CHUNKS):
                z1(i, k).wait_send()

    p0_d().wait_send()
    for k in range(1, 4):
        y1_d(k).wait_send()
        x1_d(k).wait_send()
    for j in range(4):
        p0(j).wait_send()
    for i in range(CHUNKS):
        for k in range(1, 4):
            for make in (y1, x1, x2, y2):
                make(i, k).wait_send()
        for k in range(4):
            p2(i, k).wait_send()


def store_kernel(values, proj, y_out, du_out, db_out, dc_out, sem):
    moves = ((values.at[0], y_out), (values.at[1], du_out), (proj.at[1], db_out), (proj.at[0], dc_out))
    copies = [pltpu.make_async_copy(src, dst, sem.at[i]) for i, (src, dst) in enumerate(moves)]
    for one in copies:
        one.start()
    for one in copies:
        one.wait()


def body(layer_input, cotangent, b_proj, c_proj, log_decay, resets, agent_ids, skip_gain, agent_table):
    dma = pltpu.SemaphoreType.DMA
    vm = pltpu.VMEM
    any_spec = pl.BlockSpec(memory_space=pl.ANY)
    vmem_spec = pl.BlockSpec(memory_space=pltpu.VMEM)
    wide = (TOK, FEAT)
    n = CHUNKS
    hbm = [
        pltpu.with_memory_space_constraint(a, pltpu.HBM)
        for a in (layer_input, cotangent, b_proj, c_proj, log_decay.T, agent_table)
    ]
    values, proj = pl.pallas_call(
        kernel,
        out_shape=(vm((2, TOK, FEAT), BF16), vm((2, TOK, STATE), BF16)),
        in_specs=[any_spec] * 6 + [vmem_spec] * 2 + [pl.BlockSpec(memory_space=pltpu.SMEM)],
        out_specs=(vmem_spec, vmem_spec),
        scratch_shapes=[
            vm(wide, BF16), vm(wide, BF16), vm((2, TOK, STATE), BF16), vm((2, STATE, TOK), BF16),
            vm((8, 8, TOK), F32), vm((8, 64, GROUP), BF16), vm((8, 8, TOK), F32),
            vm((TOK, TOK), F32), vm((TOK, TOK), F32), vm((TOK, TOK), F32),
            vm((TOK, 64), BF16), vm((2, TOK, 192), BF16), vm((192, FEAT), BF16),
            vm(wide, BF16), vm((2, TOK, FEAT), BF16), vm((2, TOK, FEAT), F32), vm((2, TOK, FEAT), F32),
            vm((2, TOK, STATE), F32),
            vm((2, 4, STATE, SLICE), BF16), vm((1, FEAT), F32), vm((4, STATE, SLICE), BF16), vm((1, FEAT), F32),
            vm((4, STATE, SLICE), BF16), vm((4, 1, SLICE), F32),
            vm((4, STATE, SLICE), BF16), vm((4, 1, SLICE), F32), vm((3, STATE, SLICE), F32),
            vm((STATE, SLICE), BF16), vm((1, SLICE), F32),
            vm((n, 4, PIECE, SLICE), BF16), vm((4, 1, SLICE), F32), vm((n, 3, PIECE, SLICE), F32),
            vm((n, PIECE, SLICE), BF16), vm((1, SLICE), F32),
            vm((n, 7, PIECE, SLICE), BF16), vm((7, 1, SLICE), F32),
            vm((n, 4, PIECE, SLICE), BF16), vm((STATE, SLICE), BF16),
            vm((4, STATE, SLICE), BF16), vm((4, STATE, SLICE), BF16), vm((2, 4, STATE, SLICE), BF16),
            dma((6,)), dma((2, 7)), dma((2, 7)), dma((4,)), dma((4,)), dma((1,)), dma((1,)),
            dma((n, 3)), dma((n, 3)), dma((3,)), dma((3,)),
            dma((n, 3)), dma((n, 3)), dma((3,)), dma((3,)),
            dma((n, 7)), dma((n, 7)), dma((7,)), dma((7,)),
            dma((n, 3)), dma((n, 3)), dma((n, 3)), dma((n, 3)), dma((n, 4)), dma((n, 4)),
            pltpu.SemaphoreType.REGULAR, vm((6, 8 * TOK), F32),
        ],
        compiler_params=pltpu.CompilerParams(
            collective_id=0, has_side_effects=True, vmem_limit_bytes=56 * 1024 * 1024
        ),
        name="tract_scan",
    )(*hbm, resets.reshape(1, -1), agent_ids.reshape(1, -1), skip_gain)
    token = jax.ShapeDtypeStruct(wide, BF16)
    narrow = jax.ShapeDtypeStruct((TOK, STATE), BF16)
    return pl.pallas_call(
        store_kernel,
        out_shape=(token, token, narrow, narrow),
        in_specs=[any_spec] * 2,
        out_specs=(any_spec,) * 4,
        scratch_shapes=[dma((4,))],
        name="store",
    )(pltpu.with_memory_space_constraint(values, vm), pltpu.with_memory_space_constraint(proj, vm))


def solution(mesh):
    return jax.shard_map(
        body,
        mesh=mesh,
        in_specs=(
            P(("ctx", "head"), None),
            P(("ctx", "head"), None),
            P("ctx", None),
            P("ctx", None),
            P("ctx", "head"),
            P("ctx"),
            P("ctx"),
            P(),
            P(None, "head"),
        ),
        out_specs=(P(("ctx", "head"), None),) * 4,
        check_vma=False,
    )
```

time: 654 us -> 58.1 us (0.09)
  waiting for transfers between devices: 180 us -> 0 us
  matrix products: 149 us -> 0 us
  other arithmetic: 112 us -> 0 us
  local copies, waits for them, and re-layouts: 69.9 us -> 0 us
  blocking collectives: 63.5 us -> 0 us
  Pallas kernels: 0 us -> 57.4 us
  loops' own time: 37.8 us -> 0 us
  starting transfers between devices: 21.1 us -> 0 us
  between operations: 14.7 us -> 0.64 us
    dot_general x97 -> x0, matrix products: 149 us -> none  [the longest x8 16.6 us: tract_carry(): jnp.einsum('tn,hpn->thp', c_rows.astype(jnp.float32), state_in, precision...]
    all_gather x2 -> x0, waiting for transfers between devices: 95.5 us -> none  [prefix(): gathered = jax.tree.map(lambda a: lax.all_gather(a, axis), part)]
    all_to_all x4 -> x0, waiting for transfers between devices: 75.2 us -> none  [the longest x1 22.5 us: body(): lax.all_to_all(y_tok, 'head', split_axis=0, concat_axis=1, tiled=True)]
    unnamed x1 -> x0, blocking collectives: 63.5 us -> none
    pallas_call x0 -> x2, Pallas kernels: none -> 57.4 us  [the longest x1 55.6 us: body(): pl.pallas_call(kernel, out_shape=(vm((2, TOK, FEAT), BF16), vm((2, TOK, S...]
    add x48 -> x0, other arithmetic: 52 us -> none  [the longest x47 48.1 us: link(): later[0][:, None, None] * earlier[1] + later[1]]
    another operation x6 -> x0, loops' own time: 37.8 us -> none  [the longest x1 20 us: run_core(): summaries = lax.map(summary_only, records)]
    another operation x76 -> x0, other arithmetic: 35.7 us -> none
  transfers between devices with their start and end apart: 8 -> 0, of which waited for: 7 -> 0; matrix products, arithmetic and copies ran while one was open for 6% -> 0% of each run, Pallas kernels for 0% -> 0%
where the time goes in v1:
time: 58.1 us; the launch traced here: 58 us
  Pallas kernels  57.4 us (99%)
  between operations  0.64 us (1%)
    pallas_call x1, Pallas kernels, body(): pl.pallas_call(kernel, out_shape=(vm((2, TOK, FEAT), BF16), vm((2, TOK, S...  55.6 us
    pallas_call x1, Pallas kernels, body(): pl.pallas_call(store_kernel, out_shape=(token, token, narrow, narrow), in...  1.72 us

profile of v1, /device:TPU:1, one launch (start us, length us, event | category | flops | bytes accessed | tf_op | source)
XLA Modules:
  0.0 58.0 jit_solution(11367559840543914023)
XLA Ops:
  0.6 55.6 %tract_scan.1 = (bf16[2,256,3072]{2,1,0:T(8,128)(2,1)S(1)}, bf16[2,256,128]{2,1,0:T(8,128)(2,1)S(1)}) custom-call(bf16[256,3072]{1,0:T(8,128)(2,1)} %x_hbm.1, bf16[256,3072]{1,0:T(8,128)(2,1)} %g_hbm.1, bf16[2048,128]{1,0:T(8,128)(2,1)} %b_hbm.1, bf16[2048,128]{1,0:T(8,128)(2,1)} %c_hbm.1, f32[6,2048]{1,0:T(8,128)} %bitcast.3, bf16[64,384]{1,0:T(8,128)(2,1)} %tab_hbm.1, ...), custom_call_target="tpu_custom_call" | custom-call | tf_op jit(solution)/shard_map/tract_scan/pallas_call | solution.py:542
  56.3 1.7 %store.1 = (bf16[256,3072]{1,0:T(8,128)(2,1)}, bf16[256,3072]{1,0:T(8,128)(2,1)}, bf16[256,128]{1,0:T(8,128)(2,1)}, bf16[256,128]{1,0:T(8,128)(2,1)}) custom-call(bf16[2,256,3072]{2,1,0:T(8,128)(2,1)S(1)} %get-tuple-element.6.values, bf16[2,256,128]{2,1,0:T(8,128)(2,1)S(1)} %get-tuple-element.7.proj), custom_call_target="tpu_custom_call" | custom-call | tf_op jit(solution)/shard_map/store/pallas_call | solution.py:577

commit v2 on v1

--- a/solution.py
+++ b/solution.py
@@ -18,6 +18,8 @@
 HALF = 64
 PIECE = 16
 CHUNKS = 2
+ADJOINT_AT = (1, 3, 2, 4, 5, 5, 6, 6)
+STATE_AT = (2, 4, 3, 5, 6, 7, 7, 8)
 LOG2E = 1.4426950408889634
 
 
@@ -172,16 +174,18 @@
     def columns(j):
         return pl.ds(pl.multiple_of(j * GROUP, 128), GROUP)
 
+    def slice_columns(j):
+        return pl.ds(pl.multiple_of(j * SLICE, 128), SLICE)
+
     def prepare_adjoint(j, carry):
-        cols = columns(j)
+        cols = slice_columns(j)
         weight = dot(wcat[0], spread[:, cols])
         own_d[:, cols] = weight[TOK - 1 : TOK, :]
         starts = (weight * g[:, cols].astype(F32)).astype(BF16)
-        part = pl.ds(pl.multiple_of((j % 2) * GROUP, 128), GROUP)
-        sa[1, j // 2, :, part] = dot(cbt[0], starts).astype(BF16)
+        sa[1, j] = dot(cbt[0], starts).astype(BF16)
         return carry
 
-    lax.fori_loop(0, 8, prepare_adjoint, 0)
+    lax.fori_loop(0, 4, prepare_adjoint, 0)
 
     partner = (cx, yy * 2 + 1 - core)
 
@@ -364,10 +368,13 @@
             y2(i, k).start()
         w[yy, half(i), :] = yo[pos_y, half(i), :]
 
-    def arrive(i, k):
-        if k:
-            y2(i, k).wait_recv()
-        p2(i, k).start()
+    def forward(i):
+        for k in (0, 1, 3, 2):
+            if k:
+                y2(i, k).wait_recv()
+            p2(i, k).start()
+
+    def own_carry(i, k):
         j = came(k)
         at = pl.ds(pl.multiple_of(j * SLICE, 128), SLICE)
         full[mydir, j, half(i), :] = (
@@ -385,25 +392,23 @@
         total(0)
         total(1)
 
-    def prepare_state(n, carry):
-        turn = n // 2
+    def prepare_state(turn, carry):
         step = jnp.where(turn == 0, 2, jnp.where(turn == 1, 1, jnp.where(turn == 2, 3, 0)))
         j = (yy + step) % 4
-        group = j * 2 + n % 2
-        cols = columns(group)
-        inputs = (x[:, cols].astype(F32) + dot(onehot[...], tab[group])).astype(BF16)
+        cols = slice_columns(j)
+        rows = jnp.concatenate([tab[j * 2], tab[j * 2 + 1]], axis=1)
+        inputs = (x[:, cols].astype(F32) + dot(onehot[...], rows)).astype(BF16)
         u[:, cols] = inputs
         ends = (dot(wcat[1], spread[:, cols]) * inputs.astype(F32)).astype(BF16)
-        part = pl.ds(pl.multiple_of((n % 2) * GROUP, 128), GROUP)
-        sa[0, j, :, part] = dot(cbt[1], ends).astype(BF16)
-
-        @pl.when((core == 0) & (n % 2 == 1))
+        sa[0, j] = dot(cbt[1], ends).astype(BF16)
+
+        @pl.when(core == 0)
         def _():
             p0(j).start()
 
         return carry
 
-    lax.fori_loop(0, 8, prepare_state, 0)
+    lax.fori_loop(0, 4, prepare_state, 0)
 
     @pl.when(core == 1)
     def _():
@@ -415,10 +420,14 @@
 
     def intra(j, carry):
         for adjoint_at, state_at, act, part in (
-            (2, 4, group_y, 0),
-            (4, 6, group_y, 1),
-            (4, 6, group_x, 0),
-            (6, 8, group_x, 1),
+            (ADJOINT_AT[0], STATE_AT[0], group_y, 0),
+            (ADJOINT_AT[1], STATE_AT[1], group_x, 0),
+            (ADJOINT_AT[2], STATE_AT[2], group_y, 1),
+            (ADJOINT_AT[3], STATE_AT[3], group_x, 1),
+            (ADJOINT_AT[4], STATE_AT[4], back_x, 0),
+            (ADJOINT_AT[5], STATE_AT[5], back_x, 1),
+            (ADJOINT_AT[6], STATE_AT[6], back_y, 0),
+            (ADJOINT_AT[7], STATE_AT[7], back_y, 1),
         ):
             pl.when(j == core * state_at + mydir * adjoint_at)(functools.partial(act, part))
         pl.when(j < 8)(functools.partial(local, j))
@@ -427,14 +436,15 @@
     def local(j):
         rows_l = logs[j]
         cols_l = jnp.transpose(rows_l)
+        wide = columns(j)
+        for way, values in ((0, g), (1, u)):
+            weight = dot(wcat[way], spread[:, wide])
+            wts[way, :, wide] = weight
+            gi[way, :, wide] = (weight * values[:, wide].astype(F32)).astype(BF16)
         for pair in range(3):
             cols = pl.ds(pl.multiple_of(j * GROUP + pair * 128, 128), 128)
             up = u[:, cols]
             gp = g[:, cols]
-            for way, values in ((0, gp), (1, up)):
-                weight = dot(wcat[way], spread[:, cols])
-                wts[way, :, cols] = weight
-                gi[way, :, cols] = (weight * values.astype(F32)).astype(BF16)
             zero = jnp.zeros_like(gp)
             ys, dus = [], []
             for side in range(2):
@@ -465,20 +475,17 @@
     acc[0] = dot(pairs, cb[1])
     acc[1] = dot_tn(pairs, cb[0])
 
-    back_x(0)
-    back_x(1)
-    back_y(0)
-    back_y(1)
-
     def carried_here(way):
+        forward(0)
         for k in range(4):
-            arrive(0, k)
-        for k in range(4):
-            arrive(1, k)
+            own_carry(0, k)
+        forward(1)
+        for k in (0, 1, 3, 2):
+            own_carry(1, k)
             finish(way, came(k))
 
     def carried_there(way):
-        for k in range(4):
+        for k in (0, 1, 3, 2):
             p2(0, k).wait_recv()
             p2(1, k).wait_recv()
             finish(way, at4((pos_y + k) % 4))
@@ -520,7 +527,10 @@
 
 
 def store_kernel(values, proj, y_out, du_out, db_out, dc_out, sem):
-    moves = ((values.at[0], y_out), (values.at[1], du_out), (proj.at[1], db_out), (proj.at[0], dc_out))
+    moves = [(proj.at[1], db_out), (proj.at[0], dc_out)]
+    for part in range(4):
+        rows = pl.ds(part * 64, 64)
+        moves += [(values.at[0, rows], y_out.at[rows]), (values.at[1, rows], du_out.at[rows])]
     copies = [pltpu.make_async_copy(src, dst, sem.at[i]) for i, (src, dst) in enumerate(moves)]
     for one in copies:
         one.start()
@@ -579,7 +589,7 @@
         out_shape=(token, token, narrow, narrow),
         in_specs=[any_spec] * 2,
         out_specs=(any_spec,) * 4,
-        scratch_shapes=[dma((4,))],
+        scratch_shapes=[dma((10,))],
         name="store",
     )(pltpu.with_memory_space_constraint(values, vm), pltpu.with_memory_space_constraint(proj, vm))
 

time: 58.1 us -> 56.4 us (0.971)
  Pallas kernels: 57.4 us -> 55.5 us
    pallas_call x1, Pallas kernels: 55.6 us -> 53.8 us  [body(): pl.pallas_call(kernel, out_shape=(vm((2, TOK, FEAT), BF16), vm((2, TOK, S...]
where the time goes in v2:
time: 56.4 us; the launch traced here: 56.2 us
  Pallas kernels  55.5 us (98%)
  between operations  0.64 us (1%)
    pallas_call x1, Pallas kernels, body(): pl.pallas_call(kernel, out_shape=(vm((2, TOK, FEAT), BF16), vm((2, TOK, S...  53.8 us
    pallas_call x1, Pallas kernels, body(): pl.pallas_call(store_kernel, out_shape=(token, token, narrow, narrow), in...  1.78 us

profile of v2, /device:TPU:1, one launch (start us, length us, event | category | flops | bytes accessed | tf_op | source)
XLA Modules:
  0.0 56.2 jit_solution(3989636180865513544)
XLA Ops:
  0.6 53.8 %tract_scan.1 = (bf16[2,256,3072]{2,1,0:T(8,128)(2,1)S(1)}, bf16[2,256,128]{2,1,0:T(8,128)(2,1)S(1)}) custom-call(bf16[256,3072]{1,0:T(8,128)(2,1)} %x_hbm.1, bf16[256,3072]{1,0:T(8,128)(2,1)} %g_hbm.1, bf16[2048,128]{1,0:T(8,128)(2,1)} %b_hbm.1, bf16[2048,128]{1,0:T(8,128)(2,1)} %c_hbm.1, f32[6,2048]{1,0:T(8,128)} %bitcast.3, bf16[64,384]{1,0:T(8,128)(2,1)} %tab_hbm.1, ...), custom_call_target="tpu_custom_call" | custom-call | tf_op jit(solution)/shard_map/tract_scan/pallas_call | solution.py:552
  54.4 1.8 %store.1 = (bf16[256,3072]{1,0:T(8,128)(2,1)}, bf16[256,3072]{1,0:T(8,128)(2,1)}, bf16[256,128]{1,0:T(8,128)(2,1)}, bf16[256,128]{1,0:T(8,128)(2,1)}) custom-call(bf16[2,256,3072]{2,1,0:T(8,128)(2,1)S(1)} %get-tuple-element.6.values, bf16[2,256,128]{2,1,0:T(8,128)(2,1)S(1)} %get-tuple-element.7.proj), custom_call_target="tpu_custom_call" | custom-call | tf_op jit(solution)/shard_map/store/pallas_call | solution.py:587

commit v3 on v2

--- a/solution.py
+++ b/solution.py
@@ -18,8 +18,8 @@
 HALF = 64
 PIECE = 16
 CHUNKS = 2
-ADJOINT_AT = (1, 3, 2, 4, 5, 5, 6, 6)
-STATE_AT = (2, 4, 3, 5, 6, 7, 7, 8)
+ADJOINT_AT = (1, 3, 2, 5, 5, 6, 6, 7)
+STATE_AT = (2, 4, 4, 6, 6, 7, 7, 8)
 LOG2E = 1.4426950408889634
 
 
@@ -105,6 +105,28 @@
     for one in (loads[1], loads[2], loads[0], loads[3]):
         one.start()
 
+    own_ld.wait()
+    pl.semaphore_wait(barrier, 14)
+
+    def ld_copy(k):
+        to = (hd + k) % 8
+        theirs = pl.ds(pl.multiple_of(to * TOK, TOK), TOK)
+        return remote(
+            ld_own.at[:, theirs], ld.at[hd, pl.ds(0, 6), :], hs.at[0, k - 1], hr.at[0, k - 1], (cx, to)
+        )
+
+    def tab_copy(k):
+        return remote(tab.at[hd], tab.at[hd], hs.at[1, k - 1], hr.at[1, k - 1], (cx, (hd + k) % 8))
+
+    for k in (4, 3, 5, 2, 6, 1, 7):
+        ld_copy(k).start()
+    own_tab.wait()
+    for k in (4, 3, 5, 2, 6, 1, 7):
+        tab_copy(k).start()
+    for k in (2, 6):
+        pl.semaphore_signal(ready, inc=1, device_id=(((zz + k) % 8) * 4 + xx, hd), device_id_type=MESH)
+    ld[hd, 0:6, :] = ld_own[:, mine]
+
     paired[...] = jnp.zeros_like(paired)
 
     def build(j, carry):
@@ -116,28 +138,6 @@
         return carry
 
     lax.fori_loop(0, 8, build, 0)
-    own_ld.wait()
-    own_tab.wait()
-    pl.semaphore_wait(barrier, 14)
-
-    def ld_copy(k):
-        to = (hd + k) % 8
-        theirs = pl.ds(pl.multiple_of(to * TOK, TOK), TOK)
-        return remote(
-            ld_own.at[:, theirs], ld.at[hd, pl.ds(0, 6), :], hs.at[0, k - 1], hr.at[0, k - 1], (cx, to)
-        )
-
-    def tab_copy(k):
-        return remote(tab.at[hd], tab.at[hd], hs.at[1, k - 1], hr.at[1, k - 1], (cx, (hd + k) % 8))
-
-    for k in (4, 3, 5, 2, 6, 1, 7):
-        ld_copy(k).start()
-    for k in (4, 3, 5, 2, 6, 1, 7):
-        tab_copy(k).start()
-    for k in (2, 6):
-        pl.semaphore_signal(ready, inc=1, device_id=(((zz + k) % 8) * 4 + xx, hd), device_id_type=MESH)
-    ld[hd, 0:6, :] = ld_own[:, mine]
-
     row = lax.broadcasted_iota(jnp.int32, (TOK, TOK), 0)
     col = lax.broadcasted_iota(jnp.int32, (TOK, TOK), 1)
     upper = (row <= col).astype(F32).astype(BF16)
@@ -174,6 +174,14 @@
     def columns(j):
         return pl.ds(pl.multiple_of(j * GROUP, 128), GROUP)
 
+    partner = (cx, yy * 2 + 1 - core)
+
+    def p0(j):
+        return remote(sa.at[core, j], partner_sa.at[j], ps.at[j], pr.at[j], partner)
+
+    def p0_d():
+        return remote(own_d, partner_d, pds.at[0], pdr.at[0], partner)
+
     def slice_columns(j):
         return pl.ds(pl.multiple_of(j * SLICE, 128), SLICE)
 
@@ -183,24 +191,16 @@
         own_d[:, cols] = weight[TOK - 1 : TOK, :]
         starts = (weight * g[:, cols].astype(F32)).astype(BF16)
         sa[1, j] = dot(cbt[0], starts).astype(BF16)
+
+        @pl.when(core == 1)
+        def _():
+            p0(j).start()
+
         return carry
 
     lax.fori_loop(0, 4, prepare_adjoint, 0)
 
-    partner = (cx, yy * 2 + 1 - core)
-
-    def p0(j):
-        return remote(sa.at[core, j], partner_sa.at[j], ps.at[j], pr.at[j], partner)
-
-    def p0_d():
-        return remote(own_d, partner_d, pds.at[0], pdr.at[0], partner)
-
     p0_d().start()
-
-    @pl.when(core == 1)
-    def _():
-        for j in range(4):
-            p0(j).start()
 
     loads[3].wait()
     for k in range(1, 8):
@@ -256,6 +256,15 @@
     def total(i):
         if i == 0:
             p0_d().wait_recv()
+            for k in (2, 1, 3, 0):
+                to = at4((pos_y + k) % 4)
+                at = pl.ds(pl.multiple_of(to * SLICE, 128), SLICE)
+                both = own_d[:, at] * partner_d[:, at]
+                if k:
+                    tot_d[to] = both
+                    y1_d(k).start()
+                else:
+                    yin_d[pos_y] = both
         for k in (2, 1, 3, 0):
             to = at4((pos_y + k) % 4)
             at = pl.ds(pl.multiple_of(to * SLICE, 128), SLICE)
@@ -270,19 +279,17 @@
                 y1(i, k).start()
             else:
                 yin[pos_y, half(i), :] = value
-            if i == 0:
-                both = d * partner_d[:, at]
-                if k:
-                    tot_d[to] = both
-                    y1_d(k).start()
-                else:
-                    yin_d[pos_y] = both
 
     def group_y(i):
+        if i == 0:
+            for k in (1, 3, 2):
+                y1_d(k).wait_recv()
+            gd[...] = yin_d[0] * yin_d[1] * yin_d[2] * yin_d[3]
+            for k in (2, 1, 3):
+                x1_d(k).start()
+            xin_d[pos_x] = gd[...]
         for k in (1, 3, 2):
             y1(i, k).wait_recv()
-            if i == 0:
-                y1_d(k).wait_recv()
 
         def chunk(n, carry):
             rows = piece(i, n)
@@ -294,37 +301,34 @@
             return carry
 
         lax.fori_loop(0, 4, chunk, 0)
-        if i == 0:
-            gd[...] = yin_d[0] * yin_d[1] * yin_d[2] * yin_d[3]
         for k in (2, 1, 3):
             x1(i, k).start()
+        xin[i, pos_x] = gt[piece(i, xx), :]
+
+    def group_x(i):
         if i == 0:
-            for k in (2, 1, 3):
-                x1_d(k).start()
-            xin_d[pos_x] = gd[...]
-        xin[i, pos_x] = gt[piece(i, xx), :]
-
-    def group_x(i):
+            for k in (1, 3, 2):
+                x1_d(k).wait_recv()
+            rd[...] = xin_d[0] * xin_d[1] * xin_d[2] * xin_d[3]
+            pl.semaphore_wait(ready, 2)
+            for k in (4, 3, 5, 2, 6, 1, 7):
+
+                @pl.when(pos_z + k < 8)
+                def _():
+                    z1_d(k).start()
+
         for k in (1, 3, 2):
             x1(i, k).wait_recv()
-            if i == 0:
-                x1_d(k).wait_recv()
         held = xin[i, 0].astype(F32)
         for p in range(1, 4):
             xpre[i, p - 1] = held
             held = xin_d[p] * held + xin[i, p].astype(F32)
         rt[i] = held.astype(BF16)
-        if i == 0:
-            rd[...] = xin_d[0] * xin_d[1] * xin_d[2] * xin_d[3]
-        if i == 0:
-            pl.semaphore_wait(ready, 2)
         for k in (4, 3, 5, 2, 6, 1, 7):
 
             @pl.when(pos_z + k < 8)
             def _():
                 z1(i, k).start()
-                if i == 0:
-                    z1_d(k).start()
 
     def back_x(i):
         for k in range(1, 8):

time: 56.4 us -> 55 us (0.975)
  Pallas kernels: 55.5 us -> 54.1 us
    pallas_call x1, Pallas kernels: 53.8 us -> 52.4 us  [body(): pl.pallas_call(kernel, out_shape=(vm((2, TOK, FEAT), BF16), vm((2, TOK, S...]
where the time goes in v3:
time: 55 us; the launch traced here: 54.8 us
  Pallas kernels  54.1 us (98%)
  between operations  0.64 us (1%)
    pallas_call x1, Pallas kernels, body(): pl.pallas_call(kernel, out_shape=(vm((2, TOK, FEAT), BF16), vm((2, TOK, S...  52.4 us
    pallas_call x1, Pallas kernels, body(): pl.pallas_call(store_kernel, out_shape=(token, token, narrow, narrow), in...  1.78 us

profile of v3, /device:TPU:1, one launch (start us, length us, event | category | flops | bytes accessed | tf_op | source)
XLA Modules:
  0.0 54.8 jit_solution(7766532899693863045)
XLA Ops:
  0.6 52.4 %tract_scan.1 = (bf16[2,256,3072]{2,1,0:T(8,128)(2,1)S(1)}, bf16[2,256,128]{2,1,0:T(8,128)(2,1)S(1)}) custom-call(bf16[256,3072]{1,0:T(8,128)(2,1)} %x_hbm.1, bf16[256,3072]{1,0:T(8,128)(2,1)} %g_hbm.1, bf16[2048,128]{1,0:T(8,128)(2,1)} %b_hbm.1, bf16[2048,128]{1,0:T(8,128)(2,1)} %c_hbm.1, f32[6,2048]{1,0:T(8,128)} %bitcast.3, bf16[64,384]{1,0:T(8,128)(2,1)} %tab_hbm.1, ...), custom_call_target="tpu_custom_call" | custom-call | tf_op jit(solution)/shard_map/tract_scan/pallas_call | solution.py:556
  53.0 1.8 %store.1 = (bf16[256,3072]{1,0:T(8,128)(2,1)}, bf16[256,3072]{1,0:T(8,128)(2,1)}, bf16[256,128]{1,0:T(8,128)(2,1)}, bf16[256,128]{1,0:T(8,128)(2,1)}) custom-call(bf16[2,256,3072]{2,1,0:T(8,128)(2,1)S(1)} %get-tuple-element.6.values, bf16[2,256,128]{2,1,0:T(8,128)(2,1)S(1)} %get-tuple-element.7.proj), custom_call_target="tpu_custom_call" | custom-call | tf_op jit(solution)/shard_map/store/pallas_call | solution.py:591

commit v4 on v3

--- a/solution.py
+++ b/solution.py
@@ -44,14 +44,14 @@
 
 
 def kernel(
-    x_hbm, g_hbm, b_hbm, c_hbm, ld_hbm, tab_hbm, resets_ref, ids_ref, skip_ref,
+    x_hbm, g_hbm, b_hbm, c_hbm, ld_hbm, tab_hbm, resets_hbm, ids_hbm, skip_hbm,
     out, proj_out,
     x, g, cb, cbt, ld, tab, logs, cbm, vis, paired, onehot, wcat, spread,
     u, gi, wts, loc, acc, sa, own_d, partner_sa, partner_d,
     tot, tot_d, yin, yin_d, ypre, gt, gd, xin, xin_d, xpre, rt, rd, zin, zin_d,
     xo, gc, yo, w, full,
     lsem, hs, hr, ps, pr, pds, pdr, y1s, y1r, yds, ydr, x1s, x1r, xds, xdr, z1s, z1r, zds, zdr,
-    x2s, x2r, y2s, y2r, p2s, p2r, ready, ld_own,
+    x2s, x2r, y2s, y2r, p2s, p2r, ready, ld_own, resets_ref, ids_ref, skip_ref,
 ):
     cx = lax.axis_index("ctx")
     hd = lax.axis_index("head")
@@ -100,8 +100,15 @@
         pltpu.make_async_copy(x_hbm, x, lsem.at[3]),
     ]
     own_tab = pltpu.make_async_copy(tab_hbm, tab.at[hd], lsem.at[4])
+    small = [
+        pltpu.make_async_copy(resets_hbm, resets_ref, lsem.at[6]),
+        pltpu.make_async_copy(ids_hbm, ids_ref, lsem.at[7]),
+        pltpu.make_async_copy(skip_hbm, skip_ref, lsem.at[8]),
+    ]
     own_ld.start()
     own_tab.start()
+    for one in small:
+        one.start()
     for one in (loads[1], loads[2], loads[0], loads[3]):
         one.start()
 
@@ -141,6 +148,8 @@
     row = lax.broadcasted_iota(jnp.int32, (TOK, TOK), 0)
     col = lax.broadcasted_iota(jnp.int32, (TOK, TOK), 1)
     upper = (row <= col).astype(F32).astype(BF16)
+    for one in small:
+        one.wait()
     flags = resets_ref[:, mine].astype(F32)
     seen = dot(jnp.broadcast_to(flags, (8, TOK)).astype(BF16), upper)
     seen_row = seen[0:1, :]
@@ -551,12 +560,15 @@
     n = CHUNKS
     hbm = [
         pltpu.with_memory_space_constraint(a, pltpu.HBM)
-        for a in (layer_input, cotangent, b_proj, c_proj, log_decay.T, agent_table)
+        for a in (
+            layer_input, cotangent, b_proj, c_proj, log_decay.T, agent_table,
+            resets.reshape(1, -1), agent_ids.reshape(1, -1), skip_gain,
+        )
     ]
     values, proj = pl.pallas_call(
         kernel,
         out_shape=(vm((2, TOK, FEAT), BF16), vm((2, TOK, STATE), BF16)),
-        in_specs=[any_spec] * 6 + [vmem_spec] * 2 + [pl.BlockSpec(memory_space=pltpu.SMEM)],
+        in_specs=[any_spec] * 9,
         out_specs=(vmem_spec, vmem_spec),
         scratch_shapes=[
             vm(wide, BF16), vm(wide, BF16), vm((2, TOK, STATE), BF16), vm((2, STATE, TOK), BF16),
@@ -574,18 +586,19 @@
             vm((n, 7, PIECE, SLICE), BF16), vm((7, 1, SLICE), F32),
             vm((n, 4, PIECE, SLICE), BF16), vm((STATE, SLICE), BF16),
             vm((4, STATE, SLICE), BF16), vm((4, STATE, SLICE), BF16), vm((2, 4, STATE, SLICE), BF16),
-            dma((6,)), dma((2, 7)), dma((2, 7)), dma((4,)), dma((4,)), dma((1,)), dma((1,)),
+            dma((9,)), dma((2, 7)), dma((2, 7)), dma((4,)), dma((4,)), dma((1,)), dma((1,)),
             dma((n, 3)), dma((n, 3)), dma((3,)), dma((3,)),
             dma((n, 3)), dma((n, 3)), dma((3,)), dma((3,)),
             dma((n, 7)), dma((n, 7)), dma((7,)), dma((7,)),
             dma((n, 3)), dma((n, 3)), dma((n, 3)), dma((n, 3)), dma((n, 4)), dma((n, 4)),
             pltpu.SemaphoreType.REGULAR, vm((6, 8 * TOK), F32),
+            vm((1, 8 * TOK), jnp.int32), vm((1, 8 * TOK), jnp.int32), pltpu.SMEM((48,), F32),
         ],
         compiler_params=pltpu.CompilerParams(
             collective_id=0, has_side_effects=True, vmem_limit_bytes=56 * 1024 * 1024
         ),
         name="tract_scan",
-    )(*hbm, resets.reshape(1, -1), agent_ids.reshape(1, -1), skip_gain)
+    )(*hbm)
     token = jax.ShapeDtypeStruct(wide, BF16)
     narrow = jax.ShapeDtypeStruct((TOK, STATE), BF16)
     return pl.pallas_call(

time: 55 us -> 54.7 us (level)
  no operation moved by 1% of the time
where the time goes in v4:
time: 54.7 us
  Pallas kernels  54 us (99%)
  between operations  0.64 us (1%)
    pallas_call x1, Pallas kernels, body(): pl.pallas_call(kernel, out_shape=(vm((2, TOK, FEAT), BF16), vm((2, TOK, S...  52.2 us
    pallas_call x1, Pallas kernels, body(): pl.pallas_call(store_kernel, out_shape=(token, token, narrow, narrow), in...  1.78 us

profile of v4, /device:TPU:1, one launch (start us, length us, event | category | flops | bytes accessed | tf_op | source)
XLA Modules:
  0.0 54.7 jit_solution(5108555531023918207)
XLA Ops:
  0.6 52.2 %tract_scan.1 = (bf16[2,256,3072]{2,1,0:T(8,128)(2,1)S(1)}, bf16[2,256,128]{2,1,0:T(8,128)(2,1)S(1)}) custom-call(bf16[256,3072]{1,0:T(8,128)(2,1)} %x_hbm.1, bf16[256,3072]{1,0:T(8,128)(2,1)} %g_hbm.1, bf16[2048,128]{1,0:T(8,128)(2,1)} %b_hbm.1, bf16[2048,128]{1,0:T(8,128)(2,1)} %c_hbm.1, f32[6,2048]{1,0:T(8,128)} %bitcast.3, bf16[64,384]{1,0:T(8,128)(2,1)} %tab_hbm.1, ...), custom_call_target="tpu_custom_call" | custom-call | tf_op jit(solution)/shard_map/tract_scan/pallas_call | solution.py:568
  52.9 1.8 %store.1 = (bf16[256,3072]{1,0:T(8,128)(2,1)}, bf16[256,3072]{1,0:T(8,128)(2,1)}, bf16[256,128]{1,0:T(8,128)(2,1)}, bf16[256,128]{1,0:T(8,128)(2,1)}) custom-call(bf16[2,256,3072]{2,1,0:T(8,128)(2,1)S(1)} %get-tuple-element.6.values, bf16[2,256,128]{2,1,0:T(8,128)(2,1)S(1)} %get-tuple-element.7.proj), custom_call_target="tpu_custom_call" | custom-call | tf_op jit(solution)/shard_map/store/pallas_call | solution.py:604
